TPU v7x, 32 devices: a whole 2x2x4 slice. The times are simulated.
32 devices in a mesh: band: 8 (over z, y), mem: 4 (over x, core).
Axes of the slice: x: 2, y: 2, z: 4, core: 2. Of those that a mesh axis runs over, the one named last changes fastest.
Arguments:
- ensemble: float32 [128, 5, 32, 128], P('mem', None, 'band'), may hold values from -5 to 5
- obs_value: float32 [256, 128], P(('band', 'mem')), may hold values from -6 to 6
- obs_site: int32 [256, 128], P(('band', 'mem')), may hold values from 0 to 79
- obs_count: int32 [256], P(('band', 'mem')), may hold values from 32 to 128
- obs_precision: float32 [256, 128], P(('band', 'mem')), may hold values from 0.25 to 4
- loc_weight: float32 [256, 3], P(('band', 'mem')), may hold values from 0.1 to 1
- neighbours: int32 [256, 3], P(('band', 'mem')), may hold values from 0 to 7
Outputs:
- forecast: float32 [128, 5, 32, 128], P('mem', None, 'band')
Inputs may be any that keep to these rules, and one draw needn't show every extreme that they name: `obs_site`: site v * 16 + c observes variable v at the tile's c-th cell. Slots 0 to obs_count - 1 of a tile are live. `neighbours`: entries are positions within the aligned block of 8 tiles that holds the tile.
All inputs are finite; a program needn't handle non-finite values.
Results may differ from a plain program's by a relative error of at most 0.0003.
Values sent between devices are 32-bit elements; how exact they have to be, the bound alone decides.
A program may use at most 64 MiB of HBM per device.

v0:
```python
import jax
import jax.numpy as jnp
from jax import lax
from jax.sharding import PartitionSpec as P

TILE = 16
NSI = 6
STEPS = 2
COURANT = 0.08
HIGHEST = lax.Precision.HIGHEST


def extended_2(block, sides, width):
    for axis, dim in sides:
        count = lax.axis_size(axis)
        forward = [(i, i + 1) for i in range(count - 1)]
        backward = [(target, source) for source, target in forward]
        low = lax.ppermute(
            lax.slice_in_dim(block, block.shape[dim] - width, None, axis=dim), axis, forward
        )
        high = lax.ppermute(lax.slice_in_dim(block, 0, width, axis=dim), axis, backward)
        block = jnp.concatenate([low, block, high], axis=dim)
    return block


def minmod(lower_jump, upper_jump):
    return jnp.maximum(0.0, jnp.minimum(lower_jump, upper_jump)) + jnp.minimum(
        0.0, jnp.maximum(lower_jump, upper_jump)
    )


def flux_divergence(halo_extended_field, sweep_direction, advected_field):
    extent = halo_extended_field.shape[sweep_direction]
    differences = lax.slice_in_dim(
        halo_extended_field, 1, extent, axis=sweep_direction
    ) - lax.slice_in_dim(halo_extended_field, 0, extent - 1, axis=sweep_direction)
    slopes = minmod(
        lax.slice_in_dim(differences, 0, extent - 2, axis=sweep_direction),
        lax.slice_in_dim(differences, 1, extent - 1, axis=sweep_direction),
    )
    state_left_side = lax.slice_in_dim(
        halo_extended_field, 1, extent - 2, axis=sweep_direction
    ) + 0.5 * lax.slice_in_dim(slopes, 0, extent - 3, axis=sweep_direction)
    state_right_side = lax.slice_in_dim(
        halo_extended_field, 2, extent - 1, axis=sweep_direction
    ) - 0.5 * lax.slice_in_dim(slopes, 1, extent - 2, axis=sweep_direction)
    advected_field_left = state_left_side[:, advected_field : advected_field + 1]
    advected_field_right = state_right_side[:, advected_field : advected_field + 1]
    signal_velocity = jnp.maximum(jnp.abs(advected_field_left), jnp.abs(advected_field_right))
    interface_fluxes = 0.5 * (
        advected_field_left * state_left_side + advected_field_right * state_right_side
    ) - 0.5 * signal_velocity * (state_right_side - state_left_side)
    return lax.slice_in_dim(
        interface_fluxes, 1, extent - 3, axis=sweep_direction
    ) - lax.slice_in_dim(interface_fluxes, 0, extent - 4, axis=sweep_direction)


def advance(halo_extended_field):
    centre = halo_extended_field[:, :, 2:-2]
    lat_div = flux_divergence(halo_extended_field, 2, 1)
    wrapped = jnp.concatenate([centre[..., -2:], centre, centre[..., :2]], axis=3)
    lon_div = flux_divergence(wrapped, 3, 0)
    return centre - COURANT * (lat_div + lon_div)


def obs_space(tile_state, obs_value, obs_site):
    site_count = tile_state.shape[2]
    ens_mean = jnp.mean(tile_state, axis=1)
    anomaly = tile_state - ens_mean[:, None, :]
    selector = (obs_site[:, :, None] == jnp.arange(site_count)[None, None, :]).astype(jnp.float32)
    obs_anomaly = jnp.einsum("bos,bks->bok", selector, anomaly, precision=HIGHEST)
    obs_mean = jnp.einsum("bos,bs->bo", selector, ens_mean, precision=HIGHEST)
    return (ens_mean, anomaly, obs_anomaly, obs_value - obs_mean)


def transform(local_anomaly, local_innovation, local_weight, ens_mean, anomaly):
    members = local_anomaly.shape[2]
    identity = jnp.eye(members, dtype=jnp.float32)
    weighted = local_anomaly * local_weight[:, :, None]
    gram_matrix = (
        jnp.einsum("bpk,bpj->bkj", weighted, local_anomaly, precision=HIGHEST)
        + (members - 1.0) * identity
    )
    frob_norm = jnp.sqrt(jnp.sum(gram_matrix * gram_matrix, axis=(1, 2)))
    root_iter = gram_matrix / frob_norm[:, None, None]
    inverse = jnp.broadcast_to(identity, gram_matrix.shape)
    for sweep in range(NSI):
        factor = 1.5 * identity - 0.5 * jnp.matmul(inverse, root_iter, precision=HIGHEST)
        root_iter = jnp.matmul(root_iter, factor, precision=HIGHEST)
        inverse = jnp.matmul(factor, inverse, precision=HIGHEST)
    projected = jnp.einsum("bpk,bp->bk", weighted, local_innovation, precision=HIGHEST)
    halfway = jnp.einsum("bkj,bj->bk", inverse, projected, precision=HIGHEST)
    mean_weights = (
        jnp.einsum("bkj,bj->bk", inverse, halfway, precision=HIGHEST) / frob_norm[:, None]
    )
    spread_weights = inverse * jnp.sqrt((members - 1.0) / frob_norm)[:, None, None]
    combined = spread_weights + mean_weights[:, :, None]
    return ens_mean[:, None, :] + jnp.einsum("bjk,bjs->bks", combined, anomaly, precision=HIGHEST)


def localise(obs_anomaly, innovation, slot_weight, neighbour_tiles, loc_weight, ens_mean, anomaly):
    batch_tiles = neighbour_tiles.shape[0]
    local_anomaly = obs_anomaly[neighbour_tiles].reshape(batch_tiles, -1, obs_anomaly.shape[2])
    local_innovation = innovation[neighbour_tiles].reshape(batch_tiles, -1)
    local_weight = (loc_weight[:, :, None] * slot_weight[neighbour_tiles]).reshape(batch_tiles, -1)
    return transform(local_anomaly, local_innovation, local_weight, ens_mean, anomaly)


def shards(ensemble, obs_value, obs_site, obs_count, obs_precision, loc_weight, neighbours):
    fields = ensemble
    lat_rows = fields.shape[2]
    margin = 2 * STEPS
    extended = extended_2(fields, (("band", 2),), margin)
    offset = lax.axis_index("band") * lat_rows
    lat_total = lat_rows * lax.axis_size("band")
    for repeat in range(STEPS):
        extended = advance(extended)
        remaining = margin - 2 * (repeat + 1)
        if remaining > 0:
            global_row = (
                lax.broadcasted_iota(jnp.int32, (1, 1, extended.shape[2], 1), 2)
                - remaining
                + offset
            )
            inside = (global_row >= 0) & (global_row < lat_total)
            extended = jnp.where(inside, extended, 0.0)
    fields = extended
    members, variables, lon_total = (fields.shape[0], fields.shape[1], fields.shape[3])
    flattened = fields.reshape(members, variables, lat_rows * lon_total)
    grouped = lax.all_to_all(flattened, "mem", split_axis=2, concat_axis=0, tiled=True)
    all_members = grouped.shape[0]
    tile_count = neighbours.shape[0]
    tile_state = (
        grouped.reshape(all_members, variables, tile_count, TILE)
        .transpose(2, 0, 1, 3)
        .reshape(tile_count, all_members, variables * TILE)
    )
    ens_mean, anomaly, obs_anomaly, innovation = obs_space(tile_state, obs_value, obs_site)
    live_slots = jnp.arange(obs_value.shape[1])[None, :] < obs_count[:, None]
    slot_weight = jnp.where(live_slots, obs_precision, 0.0)
    analysed = localise(
        obs_anomaly, innovation, slot_weight, neighbours, loc_weight, ens_mean, anomaly
    )
    outgoing = (
        analysed.reshape(tile_count, all_members, variables, TILE)
        .transpose(1, 2, 0, 3)
        .reshape(all_members, variables, tile_count * TILE)
    )
    returned = lax.all_to_all(outgoing, "mem", split_axis=0, concat_axis=2, tiled=True)
    fields = returned.reshape(members, variables, lat_rows, lon_total)
    return advance(extended_2(fields, (("band", 2),), 2))


def solution(mesh):
    return jax.shard_map(
        shards,
        mesh=mesh,
        in_specs=(
            P("mem", None, "band", None),
            P(("band", "mem"), None),
            P(("band", "mem"), None),
            P(("band", "mem")),
            P(("band", "mem"), None),
            P(("band", "mem"), None),
            P(("band", "mem"), None),
        ),
        out_specs=P("mem", None, "band", None),
        check_vma=False,
    )
```

profile of v0, /device:TPU:17, one launch (start us, length us, event | category | flops | bytes accessed | tf_op | source)
XLA Modules:
  0.0 91.0 jit_solution(9798595751797972321)
XLA Ops:
  0.0 1.1 %copy.23 = f32[32,5,4,128]{3,0,2,1:T(8,128)S(1)} copy(f32[32,5,4,128]{3,2,1,0:T(4,128)} %param.7) | data formatting | bytes 655360 | tf_op args[0]
  1.1 3.1 %collective-permute-start = (f32[32,5,4,128]{3,0,2,1:T(8,128)S(1)}, f32[32,5,4,128]{3,0,2,1:T(8,128)S(1)}, u32[]{:S(2)}, u32[]{:S(2)}) collective-permute-start(f32[32,5,4,128]{3,0,2,1:T(8,128)S(1)} %copy.23), channel_id=1, source_target_pairs={{0,4},{4,8},{8,12},{12,16},{16,20},{20,24},{24,28},{1,5},{5,9},{9,... | collective-permute-start | bytes 983048 | tf_op jit(solution)/shard_map/ppermute | solution.py:18
  4.2 3.0 %collective-permute-start.1 = (f32[32,5,4,128]{3,0,2,1:T(8,128)S(1)}, f32[32,5,4,128]{3,0,2,1:T(8,128)S(1)}, u32[]{:S(2)}, u32[]{:S(2)}) collective-permute-start(f32[32,5,4,128]{3,0,2,1:T(8,128)S(1)} %copy.23), channel_id=1, source_target_pairs={{4,0},{8,4},{12,8},{16,12},{20,16},{24,20},{28,24},{5,1},{9,5},{13... | collective-permute-start | bytes 983048 | tf_op jit(solution)/shard_map/ppermute | solution.py:21
  8.1 0.8 fusion.55
  9.5 0.8 copy.33
  10.3 7.3 %collective-permute-done = f32[32,5,4,128]{3,0,2,1:T(8,128)S(1)} collective-permute-done((f32[32,5,4,128]{3,0,2,1:T(8,128)S(1)}, f32[32,5,4,128]{3,0,2,1:T(8,128)S(1)}, u32[]{:S(2)}, u32[]{:S(2)}) %collective-permute-start) | collective-permute-done | bytes 327712 | tf_op jit(solution)/shard_map/ppermute | solution.py:18
  17.7 2.8 %collective-permute-done.1 = f32[32,5,4,128]{3,0,2,1:T(8,128)S(1)} collective-permute-done((f32[32,5,4,128]{3,0,2,1:T(8,128)S(1)}, f32[32,5,4,128]{3,0,2,1:T(8,128)S(1)}, u32[]{:S(2)}, u32[]{:S(2)}) %collective-permute-start.1) | collective-permute-done | bytes 327712 | tf_op jit(solution)/shard_map/ppermute | solution.py:21
  22.4 0.9 fusion.5
  27.7 1.4 %reshape.135 = f32[4,1,20480]{2,1,0:T(1,128)} reshape(f32[512,5,32]{2,1,0:T(8,128)S(1)} %bitcast.129) | data formatting | bytes 655360
  29.1 3.9 %all-to-all-start = ((f32[4,1,20480]{2,1,0:T(1,128)}), f32[4,1,20480]{2,1,0:T(1,128)S(1)}, u32[]{:S(2)}, u32[]{:S(2)}) async-start(f32[4,1,20480]{2,1,0:T(1,128)} %reshape.135), calls=%async_computation | async-start | bytes 655360 | tf_op jit(solution)/shard_map/all_to_all | solution.py:130
  34.3 4.5 %all-to-all-done = f32[4,1,20480]{2,1,0:T(1,128)S(1)} async-done(((f32[4,1,20480]{2,1,0:T(1,128)}), f32[4,1,20480]{2,1,0:T(1,128)S(1)}, u32[]{:S(2)}, u32[]{:S(2)}) %all-to-all-start) | async-done | bytes 327712 | tf_op jit(solution)/shard_map/all_to_all | solution.py:130
  39.2 1.6 %reduce.1 = f32[4,20480]{1,0:T(4,128)S(1)} reduce(f32[4,1,20480]{2,1,0:T(1,128)S(1)} %all-to-all-done, f32[]{:T(128)} %broadcast.188), dimensions={1}, to_apply=%all_to_all.22.reduce_sub_computation | reduce | bytes 655364 | tf_op jit(solution)/shard_map/all_to_all | solution.py:130
  41.5 0.8 copy.55
  45.8 2.8 %multiply_reduce_fusion = (f32[8]{0:T(128)S(1)}, f32[8,128,128]{2,1,0:T(8,128)S(1)}) fusion(f32[128,128]{1,0:T(8,128)} %fusion.52, f32[8,384,128]{2,1,0:T(8,128)S(1)} %bitcast.128, f32[8,384,128]{1,2,0:T(8,128)S(1)} %copy.34, f32[8,384]{1,0:T(8,128)S(1)} %bitcast.135), kind=kOutput, calls=%fused_computation.74 | convolution fusion | flops 604766208 | bytes 3747872 | tf_op jit(solution)/shard_map/bpk,bpj->bkj/dot_general | solution.py:81
  53.8 0.9 fusion.62
  59.5 1.8 %fusion.15 = f32[8,128,1]{1,2,0:T(1,128)S(1)} fusion(f32[8,384,1]{1,2,0:T(1,128)S(1)} %bitcast.137, f32[8,384,128]{1,2,0:T(8,128)S(1)} %copy.34, f32[8,384]{1,0:T(8,128)S(1)} %bitcast.136), kind=kOutput, calls=%fused_computation.32 | convolution fusion | flops 5111808 | bytes 1601536 | tf_op jit(solution)/shard_map/bpk,bp->bk/dot_general | solution.py:91
  62.7 0.9 %convolution_bitcast_fusion = f32[8,128,1]{1,2,0:T(1,128)S(1)} fusion(f32[8,128,128]{2,1,0:T(8,128)S(1)} %fusion.68, f32[8,128,1]{1,2,0:T(1,128)S(1)} %fusion.15), kind=kOutput, calls=%fused_computation.33 | convolution fusion | flops 1572864 | bytes 532480 | tf_op jit(solution)/shard_map/bkj,bj->bk/dot_general | solution.py:92
  63.6 0.9 %fusion.69 = f32[8,1,128]{2,1,0:T(1,128)S(1)} fusion(f32[8,128,128]{2,1,0:T(8,128)S(1)} %fusion.68, f32[8,128,1]{1,2,0:T(1,128)S(1)} %convolution_bitcast_fusion), kind=kOutput, calls=%fused_computation.161 | convolution fusion | flops 1572864 | bytes 532480 | tf_op jit(solution)/shard_map/bkj,bj->bk/dot_general | solution.py:94
  64.6 0.7 convolution_add_fusion
  65.6 11.2 %all_to_all.30 = f32[128,5,128]{2,1,0:T(8,128)S(1)} all-to-all(f32[128,5,128]{2,1,0:T(8,128)S(1)} %copy.36), channel_id=1, replica_groups=mesh['band'=8,'mem'=4] {'mem'}, dimensions={0} | all-to-all | bytes 655360 | tf_op jit(solution)/shard_map/all_to_all | solution.py:149
  77.0 2.3 %collective-permute-start.2 = (f32[32,5,2,128]{3,0,2,1:T(8,128)S(1)}, f32[32,5,2,128]{3,0,2,1:T(8,128)S(1)}, u32[]{:S(2)}, u32[]{:S(2)}) collective-permute-start(f32[32,5,2,128]{3,0,2,1:T(8,128)S(1)} %get-tuple-element.39), channel_id=1, source_target_pairs={{0,4},{4,8},{8,12},{12,16},{16,20},{20,24},{24,28},{1,5},{5,9},{9,... | collective-permute-start | bytes 491528 | tf_op jit(solution)/shard_map/ppermute | solution.py:18
  79.4 3.9 %collective-permute-start.3 = (f32[32,5,2,128]{3,0,2,1:T(8,128)S(1)}, f32[32,5,2,128]{3,0,2,1:T(8,128)S(1)}, u32[]{:S(2)}, u32[]{:S(2)}) collective-permute-start(f32[32,5,2,128]{3,0,2,1:T(8,128)S(1)} %get-tuple-element.40), channel_id=1, source_target_pairs={{4,0},{8,4},{12,8},{16,12},{20,16},{24,20},{28,24},{5,1},{9,5},{13... | collective-permute-start | bytes 491528 | tf_op jit(solution)/shard_map/ppermute | solution.py:21
  84.7 4.7 %collective-permute-done.3 = f32[32,5,2,128]{3,0,2,1:T(8,128)S(1)} collective-permute-done((f32[32,5,2,128]{3,0,2,1:T(8,128)S(1)}, f32[32,5,2,128]{3,0,2,1:T(8,128)S(1)}, u32[]{:S(2)}, u32[]{:S(2)}) %collective-permute-start.3) | collective-permute-done | bytes 163872 | tf_op jit(solution)/shard_map/ppermute | solution.py:21
  90.1 0.9 %copy.38 = f32[32,5,4,128]{3,2,1,0:T(4,128)} copy(f32[32,5,4,128]{3,0,2,1:T(8,128)S(1)} %fusion.38) | data formatting | bytes 655360 | tf_op jit(solution)/shard_map/sub | solution.py:63
  (112 shorter events, 27.3 us)
Async XLA Ops:
  0.0 17.7 %copy-start = (f32[32,5,4,128]{3,2,1,0:T(4,128)S(1)}, f32[32,5,4,128]{3,2,1,0:T(4,128)}, u32[]{:S(2)}) copy-start(f32[32,5,4,128]{3,2,1,0:T(4,128)} %param.7) | copy-start | bytes 983044
  1.1 16.6 %collective-permute-start = (f32[32,5,4,128]{3,0,2,1:T(8,128)S(1)}, f32[32,5,4,128]{3,0,2,1:T(8,128)S(1)}, u32[]{:S(2)}, u32[]{:S(2)}) collective-permute-start(f32[32,5,4,128]{3,0,2,1:T(8,128)S(1)} %copy.23), channel_id=1, source_target_pairs={{0,4},{4,8},{8,12},{12,16},{16,20},{20,24},{24,28},{1,5},{5,9},{9,... | collective-permute-start | bytes 983048 | tf_op jit(solution)/shard_map/ppermute | solution.py:18
  4.2 16.3 %collective-permute-start.1 = (f32[32,5,4,128]{3,0,2,1:T(8,128)S(1)}, f32[32,5,4,128]{3,0,2,1:T(8,128)S(1)}, u32[]{:S(2)}, u32[]{:S(2)}) collective-permute-start(f32[32,5,4,128]{3,0,2,1:T(8,128)S(1)} %copy.23), channel_id=1, source_target_pairs={{4,0},{8,4},{12,8},{16,12},{20,16},{24,20},{28,24},{5,1},{9,5},{13... | collective-permute-start | bytes 983048 | tf_op jit(solution)/shard_map/ppermute | solution.py:21
  29.1 9.7 %all-to-all-start = ((f32[4,1,20480]{2,1,0:T(1,128)}), f32[4,1,20480]{2,1,0:T(1,128)S(1)}, u32[]{:S(2)}, u32[]{:S(2)}) async-start(f32[4,1,20480]{2,1,0:T(1,128)} %reshape.135), calls=%async_computation | async-start | bytes 655360 | tf_op jit(solution)/shard_map/all_to_all | solution.py:130
  42.9 1.1 %copy-start.4 = (s32[8,128]{1,0:T(8,128)S(1)}, s32[8,128]{1,0:T(8,128)}, u32[]{:S(2)}) copy-start(s32[8,128]{1,0:T(8,128)} %param.9) | copy-start | bytes 12292
  43.2 0.7 copy-start.2
  45.8 2.8 %copy-start.1 = (f32[128,128]{1,0:T(8,128)S(1)}, f32[128,128]{1,0:T(8,128)}, u32[]{:S(2)}) copy-start(f32[128,128]{1,0:T(8,128)} %fusion.53) | copy-start | bytes 196612
  57.3 1.3 %copy-start.5 = (s32[8,128]{1,0:T(8,128)S(1)}, s32[8,128]{1,0:T(8,128)}, u32[]{:S(2)}) copy-start(s32[8,128]{1,0:T(8,128)} %param.9) | copy-start | bytes 12292
  57.3 1.3 %copy-start.7 = (f32[8,80,1]{1,0,2:T(8,128)S(1)}, f32[8,80,1]{1,0,2:T(8,128)}, u32[]{:S(2)}) copy-start(f32[8,80,1]{1,0,2:T(8,128)} %reshape.125) | copy-start | bytes 7684
  57.3 1.6 %copy-start.6 = (f32[8,128]{1,0:T(8,128)S(1)}, f32[8,128]{1,0:T(8,128)}, u32[]{:S(2)}) copy-start(f32[8,128]{1,0:T(8,128)} %param.8) | copy-start | bytes 12292
  62.0 2.6 %copy-start.3 = (f32[8,80]{1,0:T(8,128)S(1)}, f32[8,80]{1,0:T(8,128)}, u32[]{:S(2)}) copy-start(f32[8,80]{1,0:T(8,128)} %copy-done.2) | copy-start | bytes 7684
  77.0 7.7 %collective-permute-start.2 = (f32[32,5,2,128]{3,0,2,1:T(8,128)S(1)}, f32[32,5,2,128]{3,0,2,1:T(8,128)S(1)}, u32[]{:S(2)}, u32[]{:S(2)}) collective-permute-start(f32[32,5,2,128]{3,0,2,1:T(8,128)S(1)} %get-tuple-element.39), channel_id=1, source_target_pairs={{0,4},{4,8},{8,12},{12,16},{16,20},{20,24},{24,28},{1,5},{5,9},{9,... | collective-permute-start | bytes 491528 | tf_op jit(solution)/shard_map/ppermute | solution.py:18
  79.4 10.1 %collective-permute-start.3 = (f32[32,5,2,128]{3,0,2,1:T(8,128)S(1)}, f32[32,5,2,128]{3,0,2,1:T(8,128)S(1)}, u32[]{:S(2)}, u32[]{:S(2)}) collective-permute-start(f32[32,5,2,128]{3,0,2,1:T(8,128)S(1)} %get-tuple-element.40), channel_id=1, source_target_pairs={{4,0},{8,4},{12,8},{16,12},{20,16},{24,20},{28,24},{5,1},{9,5},{13... | collective-permute-start | bytes 491528 | tf_op jit(solution)/shard_map/ppermute | solution.py:21
where the time goes:
time: 91.5 us; the launch traced here: 91 us
  waiting for transfers between devices  19.3 us (21%)
  matrix products  19.3 us (21%)
  starting transfers between devices  16.3 us (18%)
  other arithmetic  12.6 us (14%)
  local copies, waits for them, and re-layouts  11.7 us (13%)
  blocking collectives  11.2 us (12%)
    all_to_all x1, blocking collectives, shards(): lax.all_to_all(outgoing, 'mem', split_axis=0, concat_axis=2, tiled=True)  11.2 us
    ppermute x2, waiting for transfers between devices, extended_2(): lax.ppermute(lax.slice_in_dim(block, 0, width, axis=dim), axis, backward)  7.53 us
    ppermute x2, waiting for transfers between devices, extended_2(): lax.ppermute(lax.slice_in_dim(block, block.shape[dim] - width, None, axis...  7.3 us
    ppermute x2, starting transfers between devices, extended_2(): lax.ppermute(lax.slice_in_dim(block, 0, width, axis=dim), axis, backward)  6.89 us
    ppermute x2, starting transfers between devices, extended_2(): lax.ppermute(lax.slice_in_dim(block, block.shape[dim] - width, None, axis...  5.48 us
    all_to_all x1, waiting for transfers between devices, shards(): lax.all_to_all(flattened, 'mem', split_axis=2, concat_axis=0, tiled=True)  4.47 us
    dot_general x6, matrix products, transform(): inverse = jnp.matmul(factor, inverse, precision=HIGHEST)  4.05 us
    unnamed x23, local copies, waits for them, and re-layouts  3.95 us
  transfers between devices with their start and end apart: 5, of which 4 were waited for; matrix products, arithmetic and copies ran while one was open for 6% of the time, Pallas kernels for 0%

commit v1 on v0

--- a/solution.py
+++ b/solution.py
@@ -127,7 +127,16 @@
     fields = extended
     members, variables, lon_total = (fields.shape[0], fields.shape[1], fields.shape[3])
     flattened = fields.reshape(members, variables, lat_rows * lon_total)
-    grouped = lax.all_to_all(flattened, "mem", split_axis=2, concat_axis=0, tiled=True)
+    recast_floor = lambda u: jnp.concatenate(
+        lax.all_to_all(
+            jnp.stack(jnp.split(u, lax.axis_size("mem"), axis=2), axis=0),
+            "mem",
+            split_axis=0,
+            concat_axis=0,
+        ),
+        axis=0,
+    )
+    grouped = recast_floor(flattened)
     all_members = grouped.shape[0]
     tile_count = neighbours.shape[0]
     tile_state = (

time: 91.5 us -> 87.1 us (0.952)
  local copies, waits for them, and re-layouts: 11.7 us -> 8.14 us
    unnamed x23 -> x21, local copies, waits for them, and re-layouts: 3.95 us -> 1.92 us
    all_to_all x1 -> x0, other arithmetic: 1.56 us -> none  [shards(): lax.all_to_all(flattened, 'mem', split_axis=2, concat_axis=0, tiled=True)]
    reshape x2 -> x0, local copies, waits for them, and re-layouts: 1.25 us -> none  [the longest x1 0.69 us: shards(): flattened = fields.reshape(members, variables, lat_rows * lon_total)]
  transfers between devices with their start and end apart: 5 -> 5, of which waited for: 4 -> 4; matrix products, arithmetic and copies ran while one was open for 6% -> 7% of each run, Pallas kernels for 0% -> 0%
where the time goes in v1:
time: 87.1 us; the launch traced here: 86.6 us
  waiting for transfers between devices  19.3 us (22%)
  matrix products  19.3 us (22%)
  starting transfers between devices  16.3 us (19%)
  other arithmetic  11.8 us (14%)
  blocking collectives  11.1 us (13%)
  local copies, waits for them, and re-layouts  8.14 us (9%)
    all_to_all x1, blocking collectives, shards(): lax.all_to_all(outgoing, 'mem', split_axis=0, concat_axis=2, tiled=True)  11.1 us
    ppermute x2, waiting for transfers between devices, extended_2(): lax.ppermute(lax.slice_in_dim(block, 0, width, axis=dim), axis, backward)  7.53 us
    ppermute x2, waiting for transfers between devices, extended_2(): lax.ppermute(lax.slice_in_dim(block, block.shape[dim] - width, None, axis...  7.3 us
    ppermute x2, starting transfers between devices, extended_2(): lax.ppermute(lax.slice_in_dim(block, 0, width, axis=dim), axis, backward)  6.88 us
    ppermute x2, starting transfers between devices, extended_2(): lax.ppermute(lax.slice_in_dim(block, block.shape[dim] - width, None, axis...  5.48 us
    all_to_all x1, waiting for transfers between devices, shards(): lax.all_to_all(jnp.stack(jnp.split(u, lax.axis_size('mem'), axis=2), axis...  4.47 us
    dot_general x6, matrix products, transform(): inverse = jnp.matmul(factor, inverse, precision=HIGHEST)  4.03 us
    all_to_all x1, starting transfers between devices, shards(): lax.all_to_all(jnp.stack(jnp.split(u, lax.axis_size('mem'), axis=2), axis...  3.92 us
  transfers between devices with their start and end apart: 5, of which 4 were waited for; matrix products, arithmetic and copies ran while one was open for 7% of the time, Pallas kernels for 0%

profile of v1, /device:TPU:17, one launch (start us, length us, event | category | flops | bytes accessed | tf_op | source)
XLA Modules:
  0.0 86.6 jit_solution(12158899793693394315)
XLA Ops:
  0.0 1.1 %copy.23 = f32[32,5,4,128]{3,0,2,1:T(8,128)S(1)} copy(f32[32,5,4,128]{3,2,1,0:T(4,128)} %param.7) | data formatting | bytes 655360 | tf_op args[0]
  1.1 3.1 %collective-permute-start = (f32[32,5,4,128]{3,0,2,1:T(8,128)S(1)}, f32[32,5,4,128]{3,0,2,1:T(8,128)S(1)}, u32[]{:S(2)}, u32[]{:S(2)}) collective-permute-start(f32[32,5,4,128]{3,0,2,1:T(8,128)S(1)} %copy.23), channel_id=1, source_target_pairs={{0,4},{4,8},{8,12},{12,16},{16,20},{20,24},{24,28},{1,5},{5,9},{9,... | collective-permute-start | bytes 983048 | tf_op jit(solution)/shard_map/ppermute | solution.py:18
  4.2 3.0 %collective-permute-start.1 = (f32[32,5,4,128]{3,0,2,1:T(8,128)S(1)}, f32[32,5,4,128]{3,0,2,1:T(8,128)S(1)}, u32[]{:S(2)}, u32[]{:S(2)}) collective-permute-start(f32[32,5,4,128]{3,0,2,1:T(8,128)S(1)} %copy.23), channel_id=1, source_target_pairs={{4,0},{8,4},{12,8},{16,12},{20,16},{24,20},{28,24},{5,1},{9,5},{13... | collective-permute-start | bytes 983048 | tf_op jit(solution)/shard_map/ppermute | solution.py:21
  7.3 0.7 compare_select_fusion
  8.1 0.8 fusion.56
  9.5 0.8 copy.31
  10.3 7.3 %collective-permute-done = f32[32,5,4,128]{3,0,2,1:T(8,128)S(1)} collective-permute-done((f32[32,5,4,128]{3,0,2,1:T(8,128)S(1)}, f32[32,5,4,128]{3,0,2,1:T(8,128)S(1)}, u32[]{:S(2)}, u32[]{:S(2)}) %collective-permute-start) | collective-permute-done | bytes 327712 | tf_op jit(solution)/shard_map/ppermute | solution.py:18
  17.7 2.8 %collective-permute-done.1 = f32[32,5,4,128]{3,0,2,1:T(8,128)S(1)} collective-permute-done((f32[32,5,4,128]{3,0,2,1:T(8,128)S(1)}, f32[32,5,4,128]{3,0,2,1:T(8,128)S(1)}, u32[]{:S(2)}, u32[]{:S(2)}) %collective-permute-start.1) | collective-permute-done | bytes 327712 | tf_op jit(solution)/shard_map/ppermute | solution.py:21
  22.4 0.9 %fusion.5 = (f32[32,5,8,129]{3,0,2,1:T(8,128)S(1)}, f32[32,5,8,129]{3,0,2,1:T(8,128)S(1)}) fusion(f32[32,5,8,130]{3,0,2,1:T(8,128)S(1)} %minimum_add_fusion, f32[32,5,8,128]{3,0,2,1:T(8,128)S(1)} %slice.346, f32[32,5,8,2]{3,0,2,1:T(8,128)S(1)} %get-tuple-element.18, f32[32,5,8,2]{3,0,2,1:T(8,128)S(1)} %get-tuple-element.19), kind=kLoop, calls=%fused_computation.11 | loop fusion | flops 990720 | bytes 3317760 | tf_op jit(solution)/shard_map/add | solution.py:41
  27.0 0.8 pad_maximum_fusion.12
  27.8 3.9 %all-to-all-start = ((f32[4,32,5,128]{3,1,2,0:T(8,128)}), f32[4,32,5,128]{3,1,2,0:T(8,128)S(1)}, u32[]{:S(2)}, u32[]{:S(2)}) async-start(f32[4,32,5,128]{3,1,2,0:T(8,128)} %pad_maximum_fusion.12), calls=%async_computation | async-start | bytes 655360 | tf_op jit(solution)/shard_map/all_to_all | solution.py:131
  33.0 4.5 %all-to-all-done = f32[4,32,5,128]{3,1,2,0:T(8,128)S(1)} async-done(((f32[4,32,5,128]{3,1,2,0:T(8,128)}), f32[4,32,5,128]{3,1,2,0:T(8,128)S(1)}, u32[]{:S(2)}, u32[]{:S(2)}) %all-to-all-start) | async-done | bytes 327712 | tf_op jit(solution)/shard_map/all_to_all | solution.py:131
  41.4 2.8 %multiply_reduce_fusion = (f32[8]{0:T(128)S(1)}, f32[8,128,128]{2,1,0:T(8,128)S(1)}) fusion(f32[128,128]{1,0:T(8,128)} %fusion.53, f32[8,384,128]{2,1,0:T(8,128)S(1)} %bitcast.133, f32[8,384,128]{1,2,0:T(8,128)S(1)} %copy.32, f32[8,384]{1,0:T(8,128)S(1)} %bitcast.137), kind=kOutput, calls=%fused_computation.73 | convolution fusion | flops 604766208 | bytes 3747872 | tf_op jit(solution)/shard_map/bpk,bpj->bkj/dot_general | solution.py:81
  44.8 0.7 fusion.52
  51.4 0.9 fusion.65
  55.1 1.8 %fusion.15 = f32[8,128,1]{1,2,0:T(1,128)S(1)} fusion(f32[8,384,1]{1,2,0:T(1,128)S(1)} %bitcast.139, f32[8,384,128]{1,2,0:T(8,128)S(1)} %copy.32, f32[8,384]{1,0:T(8,128)S(1)} %bitcast.138), kind=kOutput, calls=%fused_computation.31 | convolution fusion | flops 5111808 | bytes 1601536 | tf_op jit(solution)/shard_map/bpk,bp->bk/dot_general | solution.py:91
  58.3 0.9 %convolution_bitcast_fusion = f32[8,128,1]{1,2,0:T(1,128)S(1)} fusion(f32[8,128,128]{2,1,0:T(8,128)S(1)} %fusion.69, f32[8,128,1]{1,2,0:T(1,128)S(1)} %fusion.15), kind=kOutput, calls=%fused_computation.32 | convolution fusion | flops 1572864 | bytes 532480 | tf_op jit(solution)/shard_map/bkj,bj->bk/dot_general | solution.py:92
  59.2 0.9 %fusion.70 = f32[8,1,128]{2,1,0:T(1,128)S(1)} fusion(f32[8,128,128]{2,1,0:T(8,128)S(1)} %fusion.69, f32[8,128,1]{1,2,0:T(1,128)S(1)} %convolution_bitcast_fusion), kind=kOutput, calls=%fused_computation.167 | convolution fusion | flops 1572864 | bytes 532480 | tf_op jit(solution)/shard_map/bkj,bj->bk/dot_general | solution.py:94
  60.2 0.7 convolution_add_fusion
  61.2 11.1 %all_to_all.20 = f32[128,5,128]{2,1,0:T(8,128)S(1)} all-to-all(f32[128,5,128]{2,1,0:T(8,128)S(1)} %copy.34), channel_id=1, replica_groups=mesh['band'=8,'mem'=4] {'mem'}, dimensions={0} | all-to-all | bytes 655360 | tf_op jit(solution)/shard_map/all_to_all | solution.py:158
  72.6 2.3 %collective-permute-start.2 = (f32[32,5,2,128]{3,0,2,1:T(8,128)S(1)}, f32[32,5,2,128]{3,0,2,1:T(8,128)S(1)}, u32[]{:S(2)}, u32[]{:S(2)}) collective-permute-start(f32[32,5,2,128]{3,0,2,1:T(8,128)S(1)} %get-tuple-element.39), channel_id=1, source_target_pairs={{0,4},{4,8},{8,12},{12,16},{16,20},{20,24},{24,28},{1,5},{5,9},{9,... | collective-permute-start | bytes 491528 | tf_op jit(solution)/shard_map/ppermute | solution.py:18
  75.0 3.9 %collective-permute-start.3 = (f32[32,5,2,128]{3,0,2,1:T(8,128)S(1)}, f32[32,5,2,128]{3,0,2,1:T(8,128)S(1)}, u32[]{:S(2)}, u32[]{:S(2)}) collective-permute-start(f32[32,5,2,128]{3,0,2,1:T(8,128)S(1)} %get-tuple-element.40), channel_id=1, source_target_pairs={{4,0},{8,4},{12,8},{16,12},{20,16},{24,20},{28,24},{5,1},{9,5},{13... | collective-permute-start | bytes 491528 | tf_op jit(solution)/shard_map/ppermute | solution.py:21
  80.3 4.7 %collective-permute-done.3 = f32[32,5,2,128]{3,0,2,1:T(8,128)S(1)} collective-permute-done((f32[32,5,2,128]{3,0,2,1:T(8,128)S(1)}, f32[32,5,2,128]{3,0,2,1:T(8,128)S(1)}, u32[]{:S(2)}, u32[]{:S(2)}) %collective-permute-start.3) | collective-permute-done | bytes 163872 | tf_op jit(solution)/shard_map/ppermute | solution.py:21
  85.7 0.9 %copy.36 = f32[32,5,4,128]{3,2,1,0:T(4,128)} copy(f32[32,5,4,128]{3,0,2,1:T(8,128)S(1)} %fusion.38) | data formatting | bytes 655360 | tf_op jit(solution)/shard_map/sub | solution.py:63
  (109 shorter events, 24.6 us)
Async XLA Ops:
  0.0 17.7 %copy-start = (f32[32,5,4,128]{3,2,1,0:T(4,128)S(1)}, f32[32,5,4,128]{3,2,1,0:T(4,128)}, u32[]{:S(2)}) copy-start(f32[32,5,4,128]{3,2,1,0:T(4,128)} %param.7) | copy-start | bytes 983044
  1.1 16.6 %collective-permute-start = (f32[32,5,4,128]{3,0,2,1:T(8,128)S(1)}, f32[32,5,4,128]{3,0,2,1:T(8,128)S(1)}, u32[]{:S(2)}, u32[]{:S(2)}) collective-permute-start(f32[32,5,4,128]{3,0,2,1:T(8,128)S(1)} %copy.23), channel_id=1, source_target_pairs={{0,4},{4,8},{8,12},{12,16},{16,20},{20,24},{24,28},{1,5},{5,9},{9,... | collective-permute-start | bytes 983048 | tf_op jit(solution)/shard_map/ppermute | solution.py:18
  4.2 16.3 %collective-permute-start.1 = (f32[32,5,4,128]{3,0,2,1:T(8,128)S(1)}, f32[32,5,4,128]{3,0,2,1:T(8,128)S(1)}, u32[]{:S(2)}, u32[]{:S(2)}) collective-permute-start(f32[32,5,4,128]{3,0,2,1:T(8,128)S(1)} %copy.23), channel_id=1, source_target_pairs={{4,0},{8,4},{12,8},{16,12},{20,16},{24,20},{28,24},{5,1},{9,5},{13... | collective-permute-start | bytes 983048 | tf_op jit(solution)/shard_map/ppermute | solution.py:21
  27.8 9.7 %all-to-all-start = ((f32[4,32,5,128]{3,1,2,0:T(8,128)}), f32[4,32,5,128]{3,1,2,0:T(8,128)S(1)}, u32[]{:S(2)}, u32[]{:S(2)}) async-start(f32[4,32,5,128]{3,1,2,0:T(8,128)} %pad_maximum_fusion.12), calls=%async_computation | async-start | bytes 655360 | tf_op jit(solution)/shard_map/all_to_all | solution.py:131
  38.5 1.1 %copy-start.4 = (s32[8,128]{1,0:T(8,128)S(1)}, s32[8,128]{1,0:T(8,128)}, u32[]{:S(2)}) copy-start(s32[8,128]{1,0:T(8,128)} %param.9) | copy-start | bytes 12292
  38.8 0.7 copy-start.2
  41.4 2.8 %copy-start.1 = (f32[128,128]{1,0:T(8,128)S(1)}, f32[128,128]{1,0:T(8,128)}, u32[]{:S(2)}) copy-start(f32[128,128]{1,0:T(8,128)} %fusion.54) | copy-start | bytes 196612
  52.9 1.3 %copy-start.5 = (s32[8,128]{1,0:T(8,128)S(1)}, s32[8,128]{1,0:T(8,128)}, u32[]{:S(2)}) copy-start(s32[8,128]{1,0:T(8,128)} %param.9) | copy-start | bytes 12292
  52.9 1.3 %copy-start.7 = (f32[8,80,1]{1,0,2:T(8,128)S(1)}, f32[8,80,1]{1,0,2:T(8,128)}, u32[]{:S(2)}) copy-start(f32[8,80,1]{1,0,2:T(8,128)} %reshape.120) | copy-start | bytes 7684
  52.9 1.6 %copy-start.6 = (f32[8,128]{1,0:T(8,128)S(1)}, f32[8,128]{1,0:T(8,128)}, u32[]{:S(2)}) copy-start(f32[8,128]{1,0:T(8,128)} %param.8) | copy-start | bytes 12292
  57.6 2.6 %copy-start.3 = (f32[8,80]{1,0:T(8,128)S(1)}, f32[8,80]{1,0:T(8,128)}, u32[]{:S(2)}) copy-start(f32[8,80]{1,0:T(8,128)} %copy-done.2) | copy-start | bytes 7684
  72.6 7.7 %collective-permute-start.2 = (f32[32,5,2,128]{3,0,2,1:T(8,128)S(1)}, f32[32,5,2,128]{3,0,2,1:T(8,128)S(1)}, u32[]{:S(2)}, u32[]{:S(2)}) collective-permute-start(f32[32,5,2,128]{3,0,2,1:T(8,128)S(1)} %get-tuple-element.39), channel_id=1, source_target_pairs={{0,4},{4,8},{8,12},{12,16},{16,20},{20,24},{24,28},{1,5},{5,9},{9,... | collective-permute-start | bytes 491528 | tf_op jit(solution)/shard_map/ppermute | solution.py:18
  75.0 10.1 %collective-permute-start.3 = (f32[32,5,2,128]{3,0,2,1:T(8,128)S(1)}, f32[32,5,2,128]{3,0,2,1:T(8,128)S(1)}, u32[]{:S(2)}, u32[]{:S(2)}) collective-permute-start(f32[32,5,2,128]{3,0,2,1:T(8,128)S(1)} %get-tuple-element.40), channel_id=1, source_target_pairs={{4,0},{8,4},{12,8},{16,12},{20,16},{24,20},{28,24},{5,1},{9,5},{13... | collective-permute-start | bytes 491528 | tf_op jit(solution)/shard_map/ppermute | solution.py:21
